TPU v7x, 32 devices: a whole 2x2x4 slice. The times are simulated.
32 devices in a mesh: pts: 16 (over z, x, core), dom: 2 (over y).
Axes of the slice: x: 2, y: 2, z: 4, core: 2. Of those that a mesh axis runs over, the one named last changes fastest.
Arguments:
- vectors: bfloat16 [2, 4096, 768], P('dom', 'pts'), may hold values from -6 to 6
- neighbor_shards: int32 [2, 4096, 1], P('dom', 'pts'), may hold values from 0 to 15, as said below
- neighbor_locals: int32 [2, 4096, 32], P('dom', 'pts'), may hold values from 0 to 255
- partition: int32 [2, 4096], P('dom', 'pts'), may hold values from 0 to 1, as said below
Outputs:
- moved_vectors: bfloat16 [2, 4096, 768], P('dom', 'pts')
- moved_reverse: bfloat16 [2, 4096, 32], P('dom', 'pts')
- moved_join: bfloat16 [2, 4096, 32], P('dom', 'pts')
Inputs may be any that keep to these rules, and one draw needn't show every extreme that they name: `neighbor_shards`: the 1 numbers of one row are distinct, and the rows of one device come in aligned runs of 8 rows with equal numbers. Among the 256 rows of one device no number appears in more than 32 rows, and one number appears in exactly 32 rows. `partition`: for each id range, the 512 points of that range over all domains are split into 2 partitions of exactly 256 points each.
All inputs are finite; a program needn't handle non-finite values.
Results may differ from a plain program's by a relative error of at most 0.001.
Values may be sent and summed in bfloat16 or wider, within the bound.
A program may use at most 64 MiB of HBM per device.

v0:
```python
import functools

import jax
import jax.numpy as jnp
from jax import lax
from jax.experimental import pallas as pl
from jax.experimental.pallas import tpu as pltpu
from jax.sharding import PartitionSpec as P

R = 32
BIG = 1.0e9
NT = (((1,), (1,)), ((), ()))


def oddeven_pairs(count):
    pairs = []

    def merge(lo, hi, r):
        step = r * 2
        if step < hi - lo:
            merge(lo, hi, step)
            merge(lo + r, hi, step)
            pairs.extend((i, i + r) for i in range(lo + r, hi - r, step))
        else:
            pairs.append((lo, lo + r))

    def sort(lo, hi):
        if hi - lo >= 1:
            mid = lo + (hi - lo) // 2
            sort(lo, mid)
            sort(mid + 1, hi)
            merge(lo, hi, 1)

    sort(0, count - 1)
    return pairs


PAIRS = oddeven_pairs(R)


def exchange(items, i, j):
    a, b = items[i], items[j]
    items[i], items[j] = jnp.minimum(a, b), jnp.maximum(a, b)


def sort_list(items):
    items = list(items)
    for i, j in PAIRS:
        exchange(items, i, j)
    return items


def merge_low(first, second):
    items = [jnp.minimum(first[i], second[R - 1 - i]) for i in range(R)]
    half = R // 2
    while half:
        for i in range(R):
            if not i & half:
                exchange(items, i, i + half)
        half //= 2
    return items


def dot(a, b):
    return jnp.dot(a, b, preferred_element_type=jnp.float32)


def dot_nt(a, b):
    return lax.dot_general(a, b, NT, preferred_element_type=jnp.float32)


def iota(shape, dim):
    return lax.broadcasted_iota(jnp.int32, shape, dim)


def onehot(cond):
    return jnp.where(cond, 1.0, 0.0).astype(jnp.bfloat16)


def kernel(n, doms, cap, *refs):
    refs = list(refs)
    vec, shards_hbm, locs_hbm, part_hbm = refs[:4]
    refs = refs[4:]
    wide = shards_hbm.shape[0] > 1
    slot_shard_hbm = refs.pop(0) if wide else None
    out_vec, out_rows = refs[:2]
    (own_ref, shards_t, locs, part, slot_shard, sbuf, sinfo, rvec, rinfo, dvec, dpart, posn, ltile, lshard, selfid,
     onorm, dist, lists, rows, srows, drows,
     in_sem, vs_sem, vr_sem, is_sem, ir_sem, ds_sem, dr_sem, ps_sem, pr_sem, rs_sem, rr_sem) = refs[2:]
    per, depth = vec.shape
    list_len = locs.shape[0]
    groups = cap // 8
    lanes = groups * list_len
    me = lax.axis_index("pts")
    dom = lax.axis_index("dom")
    bar = pltpu.get_barrier_semaphore()
    fetches = [pltpu.make_async_copy(shards_hbm, shards_t, in_sem.at[0]),
               pltpu.make_async_copy(locs_hbm, locs, in_sem.at[1]),
               pltpu.make_async_copy(part_hbm, part, in_sem.at[2]),
               pltpu.make_async_copy(vec, own_ref, in_sem.at[3])]
    if wide:
        fetches.append(pltpu.make_async_copy(slot_shard_hbm, slot_shard, in_sem.at[4]))
    for fetch in fetches:
        fetch.start()

    def greet_pts(o, carry):
        pl.semaphore_signal(bar, inc=1, device_id={"pts": lax.rem(me + o, n)}, device_id_type=pl.DeviceIdType.MESH)
        return carry

    def greet_dom(o, carry):
        pl.semaphore_signal(bar, inc=1, device_id={"dom": lax.rem(dom + o, doms)}, device_id_type=pl.DeviceIdType.MESH)
        return carry

    lax.fori_loop(1, n, greet_pts, 0)
    lax.fori_loop(1, doms, greet_dom, 0)

    half = n // 2
    side = me // half
    local = lax.rem(me, half)

    def target(o):
        return lax.rem(side + 1 + o // half, 2) * half + lax.rem(local + o, half)

    def source(o):
        return lax.rem(side + 1 + o // half, 2) * half + lax.rem(local + half - lax.rem(o, half), half)

    order = [o for o in range(half + 1, n)] + [o * 3 % half for o in range(half)]

    for fetch in fetches:
        fetch.wait()
    own = own_ref[...]
    upper = onehot(iota((per, per), 0) < iota((per, per), 1))
    targets = iota((n, per), 0)
    member = shards_t[0:1, :] == targets
    for w in range(1, shards_t.shape[0]):
        member = member | (shards_t[w : w + 1, :] == targets)
    rank = dot(onehot(member), upper)
    posn[...] = jnp.where(member, rank, -1.0)
    tile = onehot(lax.rem(iota((list_len, lanes), 1), list_len) == iota((list_len, lanes), 0))

    def spread(ref):
        return lax.dot_general(ref[...].astype(jnp.float32).astype(jnp.bfloat16), tile, (((0,), (0,)), ((), ())),
                               preferred_element_type=jnp.float32)

    ltile[...] = (spread(locs) + 1.0).astype(jnp.bfloat16)
    if wide:
        lshard[...] = spread(slot_shard)
    lane_group = iota((8, lanes), 1) // list_len
    slot_row = iota((cap, per), 0).astype(jnp.float32)

    def fold(full):
        flat = jnp.zeros((8, lanes), jnp.float32)
        for g in range(groups):
            flat = jnp.where(lane_group == g, full[8 * g : 8 * g + 8], flat)
        return flat.astype(jnp.bfloat16)

    batch = 4

    def pack(b, carry):
        dests = [target(b * batch + t) for t in range(batch)]
        picks = [onehot(posn[pl.ds(c, 1), :] == slot_row) for c in dests]
        pick = jnp.concatenate(picks, axis=0)
        packed = dot(pick, own_ref[...]).astype(jnp.bfloat16)
        if not wide:
            full = dot(pick, ltile[...])
        for t, c in enumerate(dests):
            sbuf[c] = packed[t * cap : t * cap + cap]
            if wide:
                entry = jnp.where(lshard[...] == c.astype(jnp.float32), ltile[...].astype(jnp.float32), 0.0)
                sinfo[c] = fold(dot(picks[t], entry.astype(jnp.bfloat16)))
            else:
                sinfo[c] = fold(full[t * cap : t * cap + cap])
        return carry

    if n <= 16:
        for b in range(n // batch):
            pack(b, 0)
    else:
        lax.fori_loop(0, n // batch, pack, 0)

    pl.semaphore_wait(bar, n - 1 + doms - 1)

    def vec_copy(c, slot_s, slot_r):
        return pltpu.make_async_remote_copy(
            src_ref=sbuf.at[c], dst_ref=rvec.at[slot_r], send_sem=vs_sem.at[slot_s], recv_sem=vr_sem.at[slot_r],
            device_id={"pts": c}, device_id_type=pl.DeviceIdType.MESH)

    def info_copy(c, slot_s, slot_r):
        return pltpu.make_async_remote_copy(
            src_ref=sinfo.at[c], dst_ref=rinfo.at[slot_r], send_sem=is_sem.at[slot_s], recv_sem=ir_sem.at[slot_r],
            device_id={"pts": c}, device_id_type=pl.DeviceIdType.MESH)

    def dom_copy(c, slot_r, src, dst, send, recv):
        return pltpu.make_async_remote_copy(
            src_ref=src, dst_ref=dst.at[slot_r], send_sem=send.at[c], recv_sem=recv.at[slot_r],
            device_id={"dom": c}, device_id_type=pl.DeviceIdType.MESH)

    def send_dom(o, carry):
        c = lax.rem(dom + o, doms)
        dom_copy(c, dom, part, dpart, ps_sem, pr_sem).start()
        dom_copy(c, dom, own_ref, dvec, ds_sem, dr_sem).start()
        return carry

    for o in order:
        c = target(o)
        info_copy(c, c, me).start()
        vec_copy(c, c, me).start()
    lax.fori_loop(1, doms, send_dom, 0)

    square = jnp.square(own.astype(jnp.float32))
    high = square.astype(jnp.bfloat16)
    low = (square - high.astype(jnp.float32)).astype(jnp.bfloat16)
    ones = jnp.ones((8, depth), jnp.bfloat16)
    onorm[...] = dot_nt(ones, high) + dot_nt(ones, low)
    id_tile = (iota((per, 128), 0) + 1).astype(jnp.float32).astype(jnp.bfloat16)
    selfid[...] = dot(onehot(posn[pl.ds(me, 1), :] == slot_row), id_tile)
    rvec[me] = sbuf[me]
    rinfo[me] = sinfo[me]
    dvec[dom] = own
    dpart[dom] = part[...]
    point = (iota((8, per), 1) + 1).astype(jnp.float32)
    width = shards_t.shape[0]

    def join(s, same):
        cand = rvec[s]
        wide_cand = cand.astype(jnp.float32)
        norm = jnp.sum(wide_cand * wide_cand, axis=1, keepdims=True)
        value = (onorm[0:1, :] + norm - 2.0 * dot_nt(cand, own_ref[...])) * (1.0 / depth)
        entry = rinfo[s].astype(jnp.float32)
        reverse, joined = [], []
        for g in range(groups):
            at = g * list_len
            listed = entry[:, at : at + 1] == point
            for k in range(1, list_len):
                listed = listed | (entry[:, at + k : at + k + 1] == point)
            allowed = entry[:, at : at + 1] > 0.0
            for w in range(1, width):
                allowed = allowed | (entry[:, at + w : at + w + 1] > 0.0)
            if same:
                allowed = allowed & (selfid[8 * g : 8 * g + 8, 0:1] != point)
            block = jnp.where(allowed, value[8 * g : 8 * g + 8], BIG)
            joined.append(block)
            reverse.append(jnp.where(listed, block, BIG))
        dist[0, s] = jnp.concatenate(reverse, axis=0).astype(jnp.bfloat16)
        dist[1, s] = jnp.concatenate(joined, axis=0).astype(jnp.bfloat16)

    join(me, True)

    def take(o, carry, near=False):
        s = source(lax.rem(o + half, n) if near else lax.rem((o - half) * 3, half))
        info_copy(s, s, s).wait_recv()
        vec_copy(s, s, s).wait_recv()
        join(s, False)
        return carry

    def take_dom(o, carry):
        s = lax.rem(dom + doms - o, doms)
        dom_copy(s, s, part, dpart, ps_sem, pr_sem).wait_recv()
        dom_copy(s, s, own_ref, dvec, ds_sem, dr_sem).wait_recv()
        return carry

    def selections():
        base = jnp.zeros((8, 1), jnp.float32)
        for d in range(doms):
            here = jnp.broadcast_to(dpart[d], (8, per)) == dom
            flag = jnp.where(here, 1.0, 0.0)
            place = jnp.where(here, dot(flag.astype(jnp.bfloat16), upper) + base, -1.0)
            base = base + jnp.sum(flag, axis=1, keepdims=True)
            yield d, onehot(place[0:1, :] == iota((per, per), 0).astype(jnp.float32))

    lax.fori_loop(1, half, functools.partial(take, near=True), 0)
    lax.fori_loop(1, doms, take_dom, 0)
    total = jnp.zeros((per, depth), jnp.float32)
    for d, pick in selections():
        total = total + dot(pick, dvec[d])
    out_vec[...] = total.astype(jnp.bfloat16)
    lax.fori_loop(half, n, take, 0)

    blocks = cap // 16
    sources = R // blocks
    chunks = n // sources
    tiles = per // 128

    def sort_one(which, tile_id):
        columns = slice(tile_id * 128, tile_id * 128 + 128)

        def chunk(t):
            items = []
            for a in range(sources):
                for b in range(blocks):
                    items.append(dist[which, t * sources + a, 16 * b : 16 * b + 16, columns])
            items = [x.astype(jnp.float32) for x in sort_list(items)]
            return merge_low([x[:8] for x in items], [x[8:] for x in items])

        if chunks == 1:
            items = chunk(0)
            for i in range(R):
                lists[tile_id, i] = items[i]
        else:
            for i in range(R):
                lists[tile_id, i] = jnp.full((8, 128), BIG, jnp.float32)

            def more(t, carry):
                items = merge_low([lists[tile_id, i] for i in range(R)], chunk(t))
                for i in range(R):
                    lists[tile_id, i] = items[i]
                return carry

            lax.fori_loop(0, chunks, more, 0)

    upper_half = iota((8, 128), 0) < 4

    def both(which, carry):
        for tile_id in range(tiles):
            sort_one(which, tile_id)
        for pair in range(tiles // 2):
            first, second = [], []
            for i in range(R):
                a, b = lists[2 * pair, i], lists[2 * pair + 1, i]
                first.append(jnp.where(upper_half, a, b))
                second.append(pltpu.roll(jnp.where(upper_half, b, a), 4, 0))
            items = merge_low(first, second)
            for shift in (6, 7):
                items = merge_low(items, [pltpu.roll(x, shift, 0) for x in items])
            for i in range(R):
                x = jnp.where(items[i] < 0.5 * BIG, items[i], 0.0)
                rows[which, i : i + 1, 256 * pair : 256 * pair + 128] = x[0:1]
                rows[which, i : i + 1, 256 * pair + 128 : 256 * pair + 256] = x[4:5]
        srows[which] = rows[which].astype(jnp.bfloat16)
        return carry

    def rows_copy(c, slot_r, which):
        return pltpu.make_async_remote_copy(
            src_ref=srows.at[which], dst_ref=drows.at[slot_r, which], send_sem=rs_sem.at[which, c],
            recv_sem=rr_sem.at[which, slot_r], device_id={"dom": c}, device_id_type=pl.DeviceIdType.MESH)

    for which in range(2):
        both(which, 0)

        def send_rows(o, carry):
            rows_copy(lax.rem(dom + o, doms), dom, which).start()
            return carry

        lax.fori_loop(1, doms, send_rows, 0)
    drows[dom] = srows[...]

    def take_rows(o, carry):
        s = lax.rem(dom + doms - o, doms)
        rows_copy(s, s, 0).wait_recv()
        rows_copy(s, s, 1).wait_recv()
        return carry

    lax.fori_loop(1, doms, take_rows, 0)
    moved = jnp.zeros((2 * R, per), jnp.float32)
    for d, pick in selections():
        moved = moved + dot_nt(jnp.concatenate([drows[d, 0], drows[d, 1]], axis=0), pick)
    out_rows[...] = moved.astype(jnp.bfloat16)

    def drain_pts(o, carry):
        c = lax.rem(me + o, n)
        info_copy(c, c, me).wait_send()
        vec_copy(c, c, me).wait_send()
        return carry

    def drain_dom(o, carry):
        c = lax.rem(dom + o, doms)
        dom_copy(c, dom, part, dpart, ps_sem, pr_sem).wait_send()
        dom_copy(c, dom, own_ref, dvec, ds_sem, dr_sem).wait_send()
        rows_copy(c, dom, 0).wait_send()
        rows_copy(c, dom, 1).wait_send()
        return carry

    lax.fori_loop(1, n, drain_pts, 0)
    lax.fori_loop(1, doms, drain_dom, 0)


def place(found_vec, found_rows, out_vec, out_rev, out_join):
    out_vec[...] = found_vec[...]
    out_rev[...] = found_rows[:R]
    out_join[...] = found_rows[R:]


def solution(mesh):
    n, doms = mesh.shape["pts"], mesh.shape["dom"]

    def per_device(vectors, neighbor_shards, neighbor_locals, partition):
        per, depth = vectors.shape[1:]
        width = neighbor_shards.shape[2]
        list_len = neighbor_locals.shape[2]
        cap = per // 8
        lanes = (cap // 8) * list_len
        operands = [vectors[0], neighbor_shards[0].T, neighbor_locals[0].T, partition]
        if width > 1:
            operands.append(neighbor_shards[0].T[jnp.arange(list_len) % width])
        bf16, f32, i32 = jnp.bfloat16, jnp.float32, jnp.int32
        dma = pltpu.SemaphoreType.DMA
        vmem = pl.BlockSpec(memory_space=pltpu.VMEM)
        anywhere = pl.BlockSpec(memory_space=pltpu.HBM)
        shapes = (jax.ShapeDtypeStruct((per, depth), bf16), jax.ShapeDtypeStruct((2 * R, per), bf16))
        found_vec, found_rows = pl.pallas_call(
            functools.partial(kernel, n, doms, cap),
            out_shape=shapes,
            in_specs=[anywhere] * len(operands),
            out_specs=(vmem, vmem),
            scratch_shapes=[
                pltpu.VMEM((per, depth), bf16),
                pltpu.VMEM((width, per), i32),
                pltpu.VMEM((list_len, per), i32),
                pltpu.VMEM((1, per), i32),
                pltpu.VMEM((list_len, per), i32),
                pltpu.VMEM((n, cap, depth), bf16),
                pltpu.VMEM((n, 8, lanes), bf16),
                pltpu.VMEM((n, cap, depth), bf16),
                pltpu.VMEM((n, 8, lanes), bf16),
                pltpu.VMEM((doms, per, depth), bf16),
                pltpu.VMEM((doms, 1, per), i32),
                pltpu.VMEM((n, per), f32),
                pltpu.VMEM((per, lanes), bf16),
                pltpu.VMEM((per, lanes), f32),
                pltpu.VMEM((cap, 128), f32),
                pltpu.VMEM((8, per), f32),
                pltpu.VMEM((2, n, cap, per), bf16),
                pltpu.VMEM((per // 128, R, 8, 128), f32),
                pltpu.VMEM((2, R, per), f32),
                pltpu.VMEM((2, R, per), bf16),
                pltpu.VMEM((doms, 2, R, per), bf16),
                dma((5,)),
                dma((n,)), dma((n,)), dma((n,)), dma((n,)),
                dma((doms,)), dma((doms,)), dma((doms,)), dma((doms,)), dma((2, doms)), dma((2, doms)),
            ],
            compiler_params=pltpu.CompilerParams(
                collective_id=0, has_side_effects=True, vmem_limit_bytes=32 * 1024 * 1024),
        )(*[pltpu.with_memory_space_constraint(x, pltpu.HBM) for x in operands])
        out_vec, out_rev, out_join = pl.pallas_call(
            place,
            out_shape=(shapes[0], jax.ShapeDtypeStruct((R, per), bf16), jax.ShapeDtypeStruct((R, per), bf16)),
            in_specs=[vmem, vmem],
            out_specs=(vmem, vmem, vmem),
            compiler_params=pltpu.CompilerParams(vmem_limit_bytes=8 * 1024 * 1024),
        )(found_vec, found_rows)
        return out_vec[None], out_rev.T[None], out_join.T[None]

    return jax.shard_map(
        per_device,
        mesh=mesh,
        in_specs=(
            P("dom", "pts", None),
            P("dom", "pts", None),
            P("dom", "pts", None),
            P("dom", "pts"),
        ),
        out_specs=(P("dom", "pts", None), P("dom", "pts", None), P("dom", "pts", None)),
        check_vma=False,
    )
```

profile of v0, /device:TPU:0, one launch (start us, length us, event | category | flops | bytes accessed | tf_op | source)
XLA Modules:
  0.0 32.1 jit_solution(9988914235751100648)
XLA Ops:
  0.6 30.7 %shard_map.67 = (bf16[256,768]{1,0:T(8,128)(2,1)S(1)}, bf16[64,256]{1,0:T(8,128)(2,1)S(1)}) custom-call(bf16[256,768]{1,0:T(8,128)(2,1)} %bitcast.12, s32[1,256]{1,0:T(1,128)} %bitcast.14, s32[32,256]{1,0:T(8,128)} %bitcast.13, s32[1,256]{1,0:T(1,128)} %refs_3_.1), custom_call_target="tpu_custom_call" | custom-call | tf_op jit(solution)/shard_map/pallas_call | solution.py:400
  31.3 0.8 %shard_map.68 = (bf16[256,768]{1,0:T(8,128)(2,1)}, bf16[32,256]{1,0:T(8,128)(2,1)}, bf16[32,256]{1,0:T(8,128)(2,1)}) custom-call(bf16[256,768]{1,0:T(8,128)(2,1)S(1)} %get-tuple-element.8.found_vec, bf16[64,256]{1,0:T(8,128)(2,1)S(1)} %get-tuple-element.9.found_rows), custom_call_target="tpu_custom_call" | custom-call | tf_op jit(solution)/shard_map/pallas_call | solution.py:434
where the time goes:
time: 32.2 us; the launch traced here: 32.1 us
  Pallas kernels  31.4 us (98%)
  between operations  0.64 us (2%)
    pallas_call x1, Pallas kernels, per_device(): pl.pallas_call(functools.partial(kernel, n, doms, cap), out_shape=shapes,...  30.7 us
    pallas_call x1, Pallas kernels, per_device(): pl.pallas_call(place, out_shape=(shapes[0], jax.ShapeDtypeStruct((R, per)...  0.78 us

commit v1 on v0

v1 whole, which is shorter than its diff:
```python
import functools

import jax
import jax.numpy as jnp
from jax import lax
from jax.experimental import pallas as pl
from jax.experimental.pallas import tpu as pltpu
from jax.sharding import PartitionSpec as P

R = 32
BIG = 1.0e9
NT = (((1,), (1,)), ((), ()))

START = (0, 1, 2, 4, 3)
SORT = (
    ((0,),),
    ((1,), (1, 2), (0,)),
    ((1,), (1, 2), (1,), (0,)),
    ((0, 4), (0,), (0, 2), (0,), (1,), (1, 4), (1,)),
    ((1, 3), (1,), (1, 2), (1,), (0,), (0, 4), (0,), (0, 3), (0,)),
)
MERGE = ((0, 3), (0, 2), (0,), (0, 2), (0, 4), (1,), (0,), (0, 4), (0,), (0, 3), (0,))
FINISH = ((0, 2),)


BATCHES = (4, 4, 4, 4)
ORDER = (8, 1, 9, 2, 10, 3, 11, 4, 12, 5, 13, 6, 14, 7, 15)
WAIT = (1, 2, 3, 8, 4, 9, 5, 10, 6, 11, 7, 12, 13, 14, 15)


def dot(a, b):
    return jnp.dot(a, b, preferred_element_type=jnp.float32)


def dot_nt(a, b):
    return lax.dot_general(a, b, NT, preferred_element_type=jnp.float32)


def iota(shape, dim):
    return lax.broadcasted_iota(jnp.int32, shape, dim)


def onehot(cond):
    return jnp.where(cond, 1.0, 0.0).astype(jnp.bfloat16)


def pairs_along(bit):
    return [(i, i | 1 << bit) for i in range(4) if not i >> bit & 1]


def run_steps(items, steps, falling=False):
    items = list(items)
    place = iota(items[0].shape, 0)
    for step in steps:
        for i, j in pairs_along(step[0]):
            a, b = items[i], items[j]
            if len(step) == 1:
                low, high = jnp.minimum(a, b), jnp.maximum(a, b)
                items[i], items[j] = (high, low) if falling else (low, high)
            else:
                far = 1 << step[1] - 2
                first = (place & far) == 0
                items[i] = jnp.where(first, a, pltpu.roll(b, far, 0))
                items[j] = jnp.where(first, pltpu.roll(a, 8 - far, 0), b)
    return items


def flip(items, bits):
    place = iota(items[0].shape, 0)
    rows = [b - 2 for b in bits if b > 1]
    out = []
    for i, x in enumerate(items):
        odd = sum(i >> b & 1 for b in bits if b < 2) & 1
        if rows:
            total = sum((place >> s) & 1 for s in rows)
            sign = jnp.where((total & 1) == odd, 1.0, -1.0)
            x = x * sign
        elif odd:
            x = -x
        out.append(x)
    return out


def sort_falling(items):
    where = list(START)
    negated = None
    for phase, steps in enumerate(SORT):
        bit = phase + 1
        bits = []
        if negated is not None:
            bits.append(where.index(negated))
        negated = bit if bit < 5 else None
        if negated is not None:
            bits.append(where.index(negated))
        items = flip(items, bits)
        items = run_steps(items, steps, falling=bit == 5)
        for step in steps:
            if len(step) == 2:
                v, s = step
                where[v], where[s] = where[s], where[v]
    return items


def merge_low(rising, falling):
    return run_steps([jnp.minimum(a, b) for a, b in zip(rising, falling)], MERGE)


def kernel(n, doms, cap, order, *refs):
    refs = list(refs)
    vec, shards_hbm, locs_hbm, part_hbm = refs[:4]
    refs = refs[4:]
    wide = shards_hbm.shape[0] > 1
    slot_shard_hbm = refs.pop(0) if wide else None
    out_vec, out_rows = refs[:2]
    (own_ref, shards_t, locs, part, slot_shard, sbuf, sinfo, rvec, rinfo, dvec, dpart, posn, ltile, lshard, selfid,
     onorm, best, picks, srows, drows,
     in_sem, vs_sem, vr_sem, is_sem, ir_sem, ds_sem, dr_sem, ps_sem, pr_sem, rs_sem, rr_sem) = refs[2:]
    per, depth = vec.shape
    list_len = locs.shape[0]
    groups = cap // 8
    lanes = groups * list_len
    me = lax.axis_index("pts")
    dom = lax.axis_index("dom")
    bar = pltpu.get_barrier_semaphore()
    bits = [1 << b for b in range(n.bit_length() - 1)]

    def partner(o):
        return me + sum(lax.rem(o // b, 2) * (b - 2 * b * lax.rem(me // b, 2)) for b in bits)

    def greet_pts(o, carry):
        pl.semaphore_signal(bar, inc=1, device_id={"pts": lax.rem(me + o, n)}, device_id_type=pl.DeviceIdType.MESH)
        return carry

    def greet_dom(o, carry):
        pl.semaphore_signal(bar, inc=1, device_id={"dom": lax.rem(dom + o, doms)}, device_id_type=pl.DeviceIdType.MESH)
        return carry

    fetch_shards = pltpu.make_async_copy(shards_hbm, shards_t, in_sem.at[0])
    fetch_locs = pltpu.make_async_copy(locs_hbm, locs, in_sem.at[1])
    fetch_part = pltpu.make_async_copy(part_hbm, part, in_sem.at[2])
    fetch_vec = pltpu.make_async_copy(vec, own_ref, in_sem.at[3])
    fetch_shards.start()
    fetch_vec.start()
    fetch_locs.start()
    if wide:
        fetch_slots = pltpu.make_async_copy(slot_shard_hbm, slot_shard, in_sem.at[4])
        fetch_slots.start()
    fetch_part.start()
    lax.fori_loop(1, n, greet_pts, 0)
    lax.fori_loop(1, doms, greet_dom, 0)

    upper = onehot(iota((per, per), 0) < iota((per, per), 1))
    tile = onehot(lax.rem(iota((list_len, lanes), 1), list_len) == iota((list_len, lanes), 0))
    targets = partner(iota((n, per), 0))
    lane_group = iota((8, lanes), 1) // list_len
    slot_row = iota((cap, per), 0).astype(jnp.float32)

    fetch_shards.wait()
    member = shards_t[0:1, :] == targets
    for w in range(1, shards_t.shape[0]):
        member = member | (shards_t[w : w + 1, :] == targets)
    rank = dot(onehot(member), upper)
    posn[...] = jnp.where(member, rank, -1.0)

    def spread(ref):
        return lax.dot_general(ref[...].astype(jnp.float32).astype(jnp.bfloat16), tile, (((0,), (0,)), ((), ())),
                               preferred_element_type=jnp.float32)

    fetch_locs.wait()
    ltile[...] = (spread(locs) + 1.0).astype(jnp.bfloat16)
    if wide:
        fetch_slots.wait()
        lshard[...] = spread(slot_shard)
    fetch_vec.wait()

    def fold(full):
        flat = jnp.zeros((8, lanes), jnp.float32)
        for g in range(groups):
            flat = jnp.where(lane_group == g, full[8 * g : 8 * g + 8], flat)
        return flat.astype(jnp.bfloat16)

    def pack(slots, offsets):
        picks_ = [onehot(posn[pl.ds(o, 1), :] == slot_row) for o in offsets]
        pick = jnp.concatenate(picks_, axis=0)
        if not wide:
            full = dot(pick, ltile[...])
        packed = dot(pick, own_ref[...]).astype(jnp.bfloat16)
        for t, (i, o) in enumerate(zip(slots, offsets)):
            if wide:
                c = partner(o)
                entry = jnp.where(lshard[...] == c.astype(jnp.float32), ltile[...].astype(jnp.float32), 0.0)
                sinfo[i] = fold(dot(picks_[t], entry.astype(jnp.bfloat16)))
            else:
                sinfo[i] = fold(full[t * cap : t * cap + cap])
            sbuf[i] = packed[t * cap : t * cap + cap]

    def vec_copy(i, c):
        return pltpu.make_async_remote_copy(
            src_ref=sbuf.at[i], dst_ref=rvec.at[i], send_sem=vs_sem.at[i], recv_sem=vr_sem.at[i],
            device_id={"pts": c}, device_id_type=pl.DeviceIdType.MESH)

    def info_copy(i, c):
        return pltpu.make_async_remote_copy(
            src_ref=sinfo.at[i], dst_ref=rinfo.at[i], send_sem=is_sem.at[i], recv_sem=ir_sem.at[i],
            device_id={"pts": c}, device_id_type=pl.DeviceIdType.MESH)

    def dom_copy(c, slot_r, src, dst, send, recv):
        return pltpu.make_async_remote_copy(
            src_ref=src, dst_ref=dst.at[slot_r], send_sem=send.at[c], recv_sem=recv.at[slot_r],
            device_id={"dom": c}, device_id_type=pl.DeviceIdType.MESH)

    def send(i, o):
        c = partner(o)
        info_copy(i, c).start()
        vec_copy(i, c).start()

    def send_dom(o, carry):
        c = lax.rem(dom + o, doms)
        dom_copy(c, dom, part, dpart, ps_sem, pr_sem).start()
        dom_copy(c, dom, own_ref, dvec, ds_sem, dr_sem).start()
        return carry

    def arrived():
        fetch_part.wait()
        pl.semaphore_wait(bar, n - 1 + doms - 1)
        lax.fori_loop(1, doms, send_dom, 0)

    if order is not None:
        whole = [(1 + WAIT.index(o), o) for o in order] + [(0, 0)]
        at = 0
        for size in BATCHES:
            some = whole[at : at + size]
            at += size
            pack([i for i, _ in some], [o for _, o in some])
            if at == size:
                arrived()
            for i, o in some:
                if o:
                    send(i, o)
    else:
        def pack_loop(b, carry):
            some = [b * 4 + t for t in range(4)]
            pack(some, some)
            return carry

        def send_loop(o, carry):
            send(o, o)
            return carry

        lax.fori_loop(0, n // 4, pack_loop, 0)
        arrived()
        lax.fori_loop(1, n, send_loop, 0)
    own = own_ref[...]
    square = jnp.square(own.astype(jnp.float32))
    high = square.astype(jnp.bfloat16)
    low = (square - high.astype(jnp.float32)).astype(jnp.bfloat16)
    ones = jnp.ones((8, depth), jnp.bfloat16)
    onorm[...] = dot_nt(ones, high) + dot_nt(ones, low)
    id_tile = (iota((per, 128), 0) + 1).astype(jnp.float32).astype(jnp.bfloat16)
    selfid[...] = dot(onehot(posn[0:1, :] == slot_row), id_tile)
    dvec[dom] = own
    dpart[dom] = part[...]
    width = shards_t.shape[0]
    for which in range(2):
        for v in range(4):
            best[which, v] = jnp.full((8, per), BIG, jnp.float32)

    def join(vectors, info, same):
        cand = vectors[...]
        wide_cand = cand.astype(jnp.float32)
        norm = jnp.sum(wide_cand * wide_cand, axis=1, keepdims=True)
        value = (onorm[0:1, :] + norm - 2.0 * dot_nt(cand, own_ref[...])) * (1.0 / depth)
        entry = info[...].astype(jnp.float32)
        point = (iota((8, per), 1) + 1).astype(jnp.float32)
        reverse, joined = [], []
        for g in range(groups):
            at = g * list_len
            listed = entry[:, at : at + 1] == point
            for k in range(1, list_len):
                listed = listed | (entry[:, at + k : at + k + 1] == point)
            allowed = entry[:, at : at + 1] > 0.0
            for w in range(1, width):
                allowed = allowed | (entry[:, at + w : at + w + 1] > 0.0)
            if same:
                allowed = allowed & (selfid[8 * g : 8 * g + 8, 0:1] != point)
            block = jnp.where(allowed, value[8 * g : 8 * g + 8], BIG)
            joined.append(block)
            reverse.append(jnp.where(listed, block, BIG))
        return reverse, joined

    def add(which, block):
        items = merge_low([best[which, v] for v in range(4)], sort_falling(block))
        for v in range(4):
            best[which, v] = items[v]

    def add_both(vectors, info, same):
        blocks = join(vectors, info, same)
        for which in range(2):
            add(which, blocks[which])

    add_both(sbuf.at[0], sinfo.at[0], True)
    other = lax.rem(me + 1, n)

    def take(i, carry):
        info_copy(i, other).wait_recv()
        vec_copy(i, other).wait_recv()
        add_both(rvec.at[i], rinfo.at[i], False)
        return carry

    def take_dom(o, carry):
        s = lax.rem(dom + doms - o, doms)
        dom_copy(s, s, part, dpart, ps_sem, pr_sem).wait_recv()
        dom_copy(s, s, own_ref, dvec, ds_sem, dr_sem).wait_recv()
        return carry

    lax.fori_loop(1, n // 2, take, 0)
    lax.fori_loop(1, doms, take_dom, 0)
    base = jnp.zeros((8, 1), jnp.float32)
    total = jnp.zeros((per, depth), jnp.float32)
    for d in range(doms):
        here = jnp.broadcast_to(dpart[d], (8, per)) == dom
        flag = jnp.where(here, 1.0, 0.0)
        place = jnp.where(here, dot(flag.astype(jnp.bfloat16), upper) + base, -1.0)
        base = base + jnp.sum(flag, axis=1, keepdims=True)
        pick = onehot(place[0:1, :] == iota((per, per), 0).astype(jnp.float32))
        picks[d] = pick
        total = total + dot(pick, dvec[d])
    out_vec[...] = total.astype(jnp.bfloat16)
    lax.fori_loop(n // 2, n, take, 0)

    def rows_copy(c, slot_r, which):
        return pltpu.make_async_remote_copy(
            src_ref=srows.at[which], dst_ref=drows.at[slot_r, which], send_sem=rs_sem.at[which, c],
            recv_sem=rr_sem.at[which, slot_r], device_id={"dom": c}, device_id_type=pl.DeviceIdType.MESH)

    for which in range(2):
        items = run_steps([best[which, v] for v in range(4)], FINISH)
        items = [items[v >> 1 | (v & 1) << 1] for v in range(4)]
        rows = jnp.concatenate([jnp.where(x < 0.5 * BIG, x, 0.0) for x in items], axis=0)
        srows[which] = rows.astype(jnp.bfloat16)

        def send_rows(o, carry):
            rows_copy(lax.rem(dom + o, doms), dom, which).start()
            return carry

        lax.fori_loop(1, doms, send_rows, 0)

    def drain_pts(i, carry):
        info_copy(i, other).wait_send()
        vec_copy(i, other).wait_send()
        return carry

    def drain_dom(o, carry):
        c = lax.rem(dom + o, doms)
        dom_copy(c, dom, part, dpart, ps_sem, pr_sem).wait_send()
        dom_copy(c, dom, own_ref, dvec, ds_sem, dr_sem).wait_send()
        return carry

    lax.fori_loop(1, n, drain_pts, 0)
    lax.fori_loop(1, doms, drain_dom, 0)
    moved = dot_nt(jnp.concatenate([srows[0], srows[1]], axis=0), picks[dom])
    for o in range(1, doms):
        s = lax.rem(dom + doms - o, doms)
        rows_copy(s, s, 0).wait_recv()
        rows_copy(s, s, 1).wait_recv()
        moved = moved + dot_nt(jnp.concatenate([drows[s, 0], drows[s, 1]], axis=0), picks[s])
    out_rows[...] = moved.astype(jnp.bfloat16)
    for o in range(1, doms):
        c = lax.rem(dom + o, doms)
        rows_copy(c, dom, 0).wait_send()
        rows_copy(c, dom, 1).wait_send()


def place(found_vec, found_rows, out_vec, out_rev, out_join):
    out_vec[...] = found_vec[...]
    out_rev[...] = found_rows[:R]
    out_join[...] = found_rows[R:]


def solution(mesh):
    n, doms = mesh.shape["pts"], mesh.shape["dom"]
    order = ORDER if n == 16 else None

    def per_device(vectors, neighbor_shards, neighbor_locals, partition):
        per, depth = vectors.shape[1:]
        width = neighbor_shards.shape[2]
        list_len = neighbor_locals.shape[2]
        cap = per // 8
        lanes = (cap // 8) * list_len
        assert cap == R
        operands = [vectors[0], neighbor_shards[0].T, neighbor_locals[0].T, partition]
        if width > 1:
            operands.append(neighbor_shards[0].T[jnp.arange(list_len) % width])
        bf16, f32, i32 = jnp.bfloat16, jnp.float32, jnp.int32
        dma = pltpu.SemaphoreType.DMA
        vmem = pl.BlockSpec(memory_space=pltpu.VMEM)
        anywhere = pl.BlockSpec(memory_space=pltpu.HBM)
        shapes = (jax.ShapeDtypeStruct((per, depth), bf16), jax.ShapeDtypeStruct((2 * R, per), bf16))
        found_vec, found_rows = pl.pallas_call(
            functools.partial(kernel, n, doms, cap, order),
            out_shape=shapes,
            in_specs=[anywhere] * len(operands),
            out_specs=(vmem, vmem),
            scratch_shapes=[
                pltpu.VMEM((per, depth), bf16),
                pltpu.VMEM((width, per), i32),
                pltpu.VMEM((list_len, per), i32),
                pltpu.VMEM((1, per), i32),
                pltpu.VMEM((list_len, per), i32),
                pltpu.VMEM((n, cap, depth), bf16),
                pltpu.VMEM((n, 8, lanes), bf16),
                pltpu.VMEM((n, cap, depth), bf16),
                pltpu.VMEM((n, 8, lanes), bf16),
                pltpu.VMEM((doms, per, depth), bf16),
                pltpu.VMEM((doms, 1, per), i32),
                pltpu.VMEM((n, per), f32),
                pltpu.VMEM((per, lanes), bf16),
                pltpu.VMEM((per, lanes), f32),
                pltpu.VMEM((cap, 128), f32),
                pltpu.VMEM((8, per), f32),
                pltpu.VMEM((2, 4, 8, per), f32),
                pltpu.VMEM((doms, per, per), bf16),
                pltpu.VMEM((2, R, per), bf16),
                pltpu.VMEM((doms, 2, R, per), bf16),
                dma((5,)),
                dma((n,)), dma((n,)), dma((n,)), dma((n,)),
                dma((doms,)), dma((doms,)), dma((doms,)), dma((doms,)), dma((2, doms)), dma((2, doms)),
            ],
            compiler_params=pltpu.CompilerParams(
                collective_id=0, has_side_effects=True, vmem_limit_bytes=32 * 1024 * 1024),
        )(*[pltpu.with_memory_space_constraint(x, pltpu.HBM) for x in operands])
        out_vec, out_rev, out_join = pl.pallas_call(
            place,
            out_shape=(shapes[0], jax.ShapeDtypeStruct((R, per), bf16), jax.ShapeDtypeStruct((R, per), bf16)),
            in_specs=[vmem, vmem],
            out_specs=(vmem, vmem, vmem),
            compiler_params=pltpu.CompilerParams(vmem_limit_bytes=8 * 1024 * 1024),
        )(found_vec, found_rows)
        return out_vec[None], out_rev.T[None], out_join.T[None]

    return jax.shard_map(
        per_device,
        mesh=mesh,
        in_specs=(
            P("dom", "pts", None),
            P("dom", "pts", None),
            P("dom", "pts", None),
            P("dom", "pts"),
        ),
        out_specs=(P("dom", "pts", None), P("dom", "pts", None), P("dom", "pts", None)),
        check_vma=False,
    )
```

time: 32.2 us -> 29.1 us (0.904)
  the two profiles are of different devices: /device:TPU:0 before, /device:TPU:10 now
where the time goes in v1:
time: 29.1 us; the launch traced here: 28.9 us
  Pallas kernels  28.3 us (97%)
  between operations  0.64 us (2%)
    pallas_call x1, Pallas kernels, per_device(): pl.pallas_call(functools.partial(kernel, n, doms, cap, order), out_shape=...  27.5 us
    pallas_call x1, Pallas kernels, per_device(): pl.pallas_call(place, out_shape=(shapes[0], jax.ShapeDtypeStruct((R, per)...  0.78 us

profile of v1, /device:TPU:10, one launch (start us, length us, event | category | flops | bytes accessed | tf_op | source)
XLA Modules:
  0.0 28.9 jit_solution(11388201078280920731)
XLA Ops:
  0.6 27.5 %shard_map.67 = (bf16[256,768]{1,0:T(8,128)(2,1)S(1)}, bf16[64,256]{1,0:T(8,128)(2,1)S(1)}) custom-call(bf16[256,768]{1,0:T(8,128)(2,1)} %bitcast.12, s32[1,256]{1,0:T(1,128)} %bitcast.14, s32[32,256]{1,0:T(8,128)} %bitcast.13, s32[1,256]{1,0:T(1,128)} %refs_3_.1), custom_call_target="tpu_custom_call" | custom-call | tf_op jit(solution)/shard_map/pallas_call | solution.py:399
  28.1 0.8 %shard_map.68 = (bf16[256,768]{1,0:T(8,128)(2,1)}, bf16[32,256]{1,0:T(8,128)(2,1)}, bf16[32,256]{1,0:T(8,128)(2,1)}) custom-call(bf16[256,768]{1,0:T(8,128)(2,1)S(1)} %get-tuple-element.8.found_vec, bf16[64,256]{1,0:T(8,128)(2,1)S(1)} %get-tuple-element.9.found_rows), custom_call_target="tpu_custom_call" | custom-call | tf_op jit(solution)/shard_map/pallas_call | solution.py:432

commit v2 on v1

--- a/solution.py
+++ b/solution.py
@@ -23,9 +23,10 @@
 FINISH = ((0, 2),)
 
 
-BATCHES = (4, 4, 4, 4)
-ORDER = (8, 1, 9, 2, 10, 3, 11, 4, 12, 5, 13, 6, 14, 7, 15)
-WAIT = (1, 2, 3, 8, 4, 9, 5, 10, 6, 11, 7, 12, 13, 14, 15)
+FIRST = 3
+LATER = ((1, 2, 3, 4, 11, 5, 6, 7, 12, 14, 13, 15), (1, 2, 3, 4, 5, 6, 11, 7, 12, 13, 14, 15))
+ORDER = (8, 9, 10, 1, 2, 3, 4, 11, 5, 6, 7, 12, 13, 14, 15)
+WAIT = (8, 1, 9, 2, 3, 10, 4, 5, 11, 6, 7, 12, 13, 14, 15)
 
 
 def dot(a, b):
@@ -114,7 +115,7 @@
     out_vec, out_rows = refs[:2]
     (own_ref, shards_t, locs, part, slot_shard, sbuf, sinfo, rvec, rinfo, dvec, dpart, posn, ltile, lshard, selfid,
      onorm, best, picks, srows, drows,
-     in_sem, vs_sem, vr_sem, is_sem, ir_sem, ds_sem, dr_sem, ps_sem, pr_sem, rs_sem, rr_sem) = refs[2:]
+     in_sem, vs_sem, vr_sem, is_sem, ir_sem, ds_sem, dr_sem, ps_sem, pr_sem, rs_sem, rr_sem, seen, across, rest) = refs[2:]
     per, depth = vec.shape
     list_len = locs.shape[0]
     groups = cap // 8
@@ -125,7 +126,14 @@
     bits = [1 << b for b in range(n.bit_length() - 1)]
 
     def partner(o):
-        return me + sum(lax.rem(o // b, 2) * (b - 2 * b * lax.rem(me // b, 2)) for b in bits)
+        swap = (o // (n // 2)) * (1 - me // (n // 2))
+        out = me
+        for b in bits:
+            odd = lax.rem(o // b, 2)
+            if b == n // 4:
+                odd = odd + swap - 2 * odd * swap
+            out = out + odd * (b - 2 * b * lax.rem(me // b, 2))
+        return out
 
     def greet_pts(o, carry):
         pl.semaphore_signal(bar, inc=1, device_id={"pts": lax.rem(me + o, n)}, device_id_type=pl.DeviceIdType.MESH)
@@ -134,6 +142,22 @@
     def greet_dom(o, carry):
         pl.semaphore_signal(bar, inc=1, device_id={"dom": lax.rem(dom + o, doms)}, device_id_type=pl.DeviceIdType.MESH)
         return carry
+
+    half, quarter = n // 2, n // 4
+    side = me // half
+
+    def tell(sem, **device):
+        pl.semaphore_signal(sem, inc=1, device_id=device, device_id_type=pl.DeviceIdType.MESH)
+
+    if order is None:
+        lax.fori_loop(1, n, greet_pts, 0)
+        lax.fori_loop(1, doms, greet_dom, 0)
+    else:
+        @pl.when(side == 0)
+        def _():
+            for o in range(n - 1, 0, -1):
+                tell(bar, pts=partner(o))
+            lax.fori_loop(1, doms, greet_dom, 0)
 
     fetch_shards = pltpu.make_async_copy(shards_hbm, shards_t, in_sem.at[0])
     fetch_locs = pltpu.make_async_copy(locs_hbm, locs, in_sem.at[1])
@@ -146,8 +170,13 @@
         fetch_slots = pltpu.make_async_copy(slot_shard_hbm, slot_shard, in_sem.at[4])
         fetch_slots.start()
     fetch_part.start()
-    lax.fori_loop(1, n, greet_pts, 0)
-    lax.fori_loop(1, doms, greet_dom, 0)
+    if order is not None:
+        @pl.when(side == 1)
+        def _():
+            pl.semaphore_wait(bar, half)
+            for o in range(half, n):
+                tell(seen.at[lax.rem(me // quarter, 2)], pts=partner(o))
+
 
     upper = onehot(iota((per, per), 0) < iota((per, per), 1))
     tile = onehot(lax.rem(iota((list_len, lanes), 1), list_len) == iota((list_len, lanes), 0))
@@ -166,11 +195,13 @@
         return lax.dot_general(ref[...].astype(jnp.float32).astype(jnp.bfloat16), tile, (((0,), (0,)), ((), ())),
                                preferred_element_type=jnp.float32)
 
-    fetch_locs.wait()
-    ltile[...] = (spread(locs) + 1.0).astype(jnp.bfloat16)
-    if wide:
-        fetch_slots.wait()
-        lshard[...] = spread(slot_shard)
+    def tile_lists():
+        fetch_locs.wait()
+        ltile[...] = (spread(locs) + 1.0).astype(jnp.bfloat16)
+        if wide:
+            fetch_slots.wait()
+            lshard[...] = spread(slot_shard)
+
     fetch_vec.wait()
 
     def fold(full):
@@ -179,20 +210,25 @@
             flat = jnp.where(lane_group == g, full[8 * g : 8 * g + 8], flat)
         return flat.astype(jnp.bfloat16)
 
-    def pack(slots, offsets):
-        picks_ = [onehot(posn[pl.ds(o, 1), :] == slot_row) for o in offsets]
-        pick = jnp.concatenate(picks_, axis=0)
+    def picks_of(offsets):
+        return [onehot(posn[pl.ds(o, 1), :] == slot_row) for o in offsets]
+
+    def pack_vec(slots, offsets):
+        packed = dot(jnp.concatenate(picks_of(offsets), axis=0), own_ref[...]).astype(jnp.bfloat16)
+        for t, i in enumerate(slots):
+            sbuf[i] = packed[t * cap : t * cap + cap]
+
+    def pack_info(slots, offsets):
+        chosen = picks_of(offsets)
         if not wide:
-            full = dot(pick, ltile[...])
-        packed = dot(pick, own_ref[...]).astype(jnp.bfloat16)
+            full = dot(jnp.concatenate(chosen, axis=0), ltile[...])
         for t, (i, o) in enumerate(zip(slots, offsets)):
             if wide:
                 c = partner(o)
                 entry = jnp.where(lshard[...] == c.astype(jnp.float32), ltile[...].astype(jnp.float32), 0.0)
-                sinfo[i] = fold(dot(picks_[t], entry.astype(jnp.bfloat16)))
+                sinfo[i] = fold(dot(chosen[t], entry.astype(jnp.bfloat16)))
             else:
                 sinfo[i] = fold(full[t * cap : t * cap + cap])
-            sbuf[i] = packed[t * cap : t * cap + cap]
 
     def vec_copy(i, c):
         return pltpu.make_async_remote_copy(
@@ -209,10 +245,8 @@
             src_ref=src, dst_ref=dst.at[slot_r], send_sem=send.at[c], recv_sem=recv.at[slot_r],
             device_id={"dom": c}, device_id_type=pl.DeviceIdType.MESH)
 
-    def send(i, o):
-        c = partner(o)
-        info_copy(i, c).start()
-        vec_copy(i, c).start()
+    def send(copy, i, o):
+        copy(i, partner(o)).start()
 
     def send_dom(o, carry):
         c = lax.rem(dom + o, doms)
@@ -227,29 +261,70 @@
 
     if order is not None:
         whole = [(1 + WAIT.index(o), o) for o in order] + [(0, 0)]
-        at = 0
-        for size in BATCHES:
-            some = whole[at : at + size]
-            at += size
+        first, others = whole[:FIRST], whole[FIRST:]
+
+        def pack_some(pack, some):
             pack([i for i, _ in some], [o for _, o in some])
-            if at == size:
-                arrived()
-            for i, o in some:
-                if o:
-                    send(i, o)
+
+        pack_some(pack_vec, first)
+
+        @pl.when(side == 0)
+        def _():
+            pl.semaphore_wait(bar, half - 1 + doms - 1)
+            pl.semaphore_wait(seen.at[1 - lax.rem(me // quarter, 2)], quarter)
+
+        for i, o in first:
+            send(vec_copy, i, o)
+        tile_lists()
+        pack_some(pack_info, whole)
+        for i, o in first:
+            send(info_copy, i, o)
+        for at in range(0, len(others), 4):
+            pack_some(pack_vec, others[at : at + 4])
+        fetch_part.wait()
+
+        @pl.when(side == 0)
+        def _():
+            pl.semaphore_wait(seen.at[lax.rem(me // quarter, 2)], quarter)
+            for o in range(1, doms):
+                tell(across, dom=lax.rem(dom + o, doms))
+
+        @pl.when(side == 1)
+        def _():
+            pl.semaphore_wait(rest, 1)
+
+        lax.fori_loop(1, doms, send_dom, 0)
+        for number, later in enumerate(LATER):
+            @pl.when(side == number)
+            def _():
+                for o in later:
+                    send(info_copy, 1 + WAIT.index(o), o)
+                    send(vec_copy, 1 + WAIT.index(o), o)
+
+
+        @pl.when(side == 0)
+        def _():
+            pl.semaphore_wait(across, doms - 1)
+            tell(rest, pts=me + half)
+
     else:
+        tile_lists()
+
         def pack_loop(b, carry):
             some = [b * 4 + t for t in range(4)]
-            pack(some, some)
+            pack_vec(some, some)
+            pack_info(some, some)
             return carry
 
         def send_loop(o, carry):
-            send(o, o)
+            send(info_copy, o, o)
+            send(vec_copy, o, o)
             return carry
 
         lax.fori_loop(0, n // 4, pack_loop, 0)
         arrived()
         lax.fori_loop(1, n, send_loop, 0)
+
     own = own_ref[...]
     square = jnp.square(own.astype(jnp.float32))
     high = square.astype(jnp.bfloat16)
@@ -326,7 +401,10 @@
         picks[d] = pick
         total = total + dot(pick, dvec[d])
     out_vec[...] = total.astype(jnp.bfloat16)
-    lax.fori_loop(n // 2, n, take, 0)
+    lax.fori_loop(n // 2, n - 1, take, 0)
+    info_copy(n - 1, other).wait_recv()
+    vec_copy(n - 1, other).wait_recv()
+    blocks = join(rvec.at[n - 1], rinfo.at[n - 1], False)
 
     def rows_copy(c, slot_r, which):
         return pltpu.make_async_remote_copy(
@@ -334,7 +412,8 @@
             recv_sem=rr_sem.at[which, slot_r], device_id={"dom": c}, device_id_type=pl.DeviceIdType.MESH)
 
     for which in range(2):
-        items = run_steps([best[which, v] for v in range(4)], FINISH)
+        items = merge_low([best[which, v] for v in range(4)], sort_falling(blocks[which]))
+        items = run_steps(items, FINISH)
         items = [items[v >> 1 | (v & 1) << 1] for v in range(4)]
         rows = jnp.concatenate([jnp.where(x < 0.5 * BIG, x, 0.0) for x in items], axis=0)
         srows[which] = rows.astype(jnp.bfloat16)
@@ -425,6 +504,7 @@
                 dma((5,)),
                 dma((n,)), dma((n,)), dma((n,)), dma((n,)),
                 dma((doms,)), dma((doms,)), dma((doms,)), dma((doms,)), dma((2, doms)), dma((2, doms)),
+                pltpu.SemaphoreType.REGULAR((2,)), pltpu.SemaphoreType.REGULAR, pltpu.SemaphoreType.REGULAR,
             ],
             compiler_params=pltpu.CompilerParams(
                 collective_id=0, has_side_effects=True, vmem_limit_bytes=32 * 1024 * 1024),

time: 29.1 us -> 28.8 us (0.990)
  the two profiles are of different devices: /device:TPU:10 before, /device:TPU:24 now
where the time goes in v2:
time: 28.8 us; the launch traced here: 28.7 us
  Pallas kernels  28.1 us (98%)
  between operations  0.64 us (2%)
    pallas_call x1, Pallas kernels, per_device(): pl.pallas_call(functools.partial(kernel, n, doms, cap, order), out_shape=...  27.3 us
    pallas_call x1, Pallas kernels, per_device(): pl.pallas_call(place, out_shape=(shapes[0], jax.ShapeDtypeStruct((R, per)...  0.78 us

profile of v2, /device:TPU:24, one launch (start us, length us, event | category | flops | bytes accessed | tf_op | source)
XLA Modules:
  0.0 28.7 jit_solution(3457921634357303253)
XLA Ops:
  0.6 27.3 %shard_map.67 = (bf16[256,768]{1,0:T(8,128)(2,1)S(1)}, bf16[64,256]{1,0:T(8,128)(2,1)S(1)}) custom-call(bf16[256,768]{1,0:T(8,128)(2,1)} %bitcast.12, s32[1,256]{1,0:T(1,128)} %bitcast.14, s32[32,256]{1,0:T(8,128)} %bitcast.13, s32[1,256]{1,0:T(1,128)} %refs_3_.1), custom_call_target="tpu_custom_call" | custom-call | tf_op jit(solution)/shard_map/pallas_call | solution.py:478
  27.9 0.8 %shard_map.68 = (bf16[256,768]{1,0:T(8,128)(2,1)}, bf16[32,256]{1,0:T(8,128)(2,1)}, bf16[32,256]{1,0:T(8,128)(2,1)}) custom-call(bf16[256,768]{1,0:T(8,128)(2,1)S(1)} %get-tuple-element.8.found_vec, bf16[64,256]{1,0:T(8,128)(2,1)S(1)} %get-tuple-element.9.found_rows), custom_call_target="tpu_custom_call" | custom-call | tf_op jit(solution)/shard_map/pallas_call | solution.py:512

commit v3 on v2

--- a/solution.py
+++ b/solution.py
@@ -340,14 +340,10 @@
         for v in range(4):
             best[which, v] = jnp.full((8, per), BIG, jnp.float32)
 
-    def join(vectors, info, same):
-        cand = vectors[...]
-        wide_cand = cand.astype(jnp.float32)
-        norm = jnp.sum(wide_cand * wide_cand, axis=1, keepdims=True)
-        value = (onorm[0:1, :] + norm - 2.0 * dot_nt(cand, own_ref[...])) * (1.0 / depth)
+    def join(vectors, info, same, arrive=None):
         entry = info[...].astype(jnp.float32)
         point = (iota((8, per), 1) + 1).astype(jnp.float32)
-        reverse, joined = [], []
+        masks = []
         for g in range(groups):
             at = g * list_len
             listed = entry[:, at : at + 1] == point
@@ -358,6 +354,15 @@
                 allowed = allowed | (entry[:, at + w : at + w + 1] > 0.0)
             if same:
                 allowed = allowed & (selfid[8 * g : 8 * g + 8, 0:1] != point)
+            masks.append((listed, allowed))
+        if arrive is not None:
+            arrive.wait_recv()
+        cand = vectors[...]
+        wide_cand = cand.astype(jnp.float32)
+        norm = jnp.sum(wide_cand * wide_cand, axis=1, keepdims=True)
+        value = (onorm[0:1, :] + norm - 2.0 * dot_nt(cand, own_ref[...])) * (1.0 / depth)
+        reverse, joined = [], []
+        for g, (listed, allowed) in enumerate(masks):
             block = jnp.where(allowed, value[8 * g : 8 * g + 8], BIG)
             joined.append(block)
             reverse.append(jnp.where(listed, block, BIG))
@@ -403,8 +408,7 @@
     out_vec[...] = total.astype(jnp.bfloat16)
     lax.fori_loop(n // 2, n - 1, take, 0)
     info_copy(n - 1, other).wait_recv()
-    vec_copy(n - 1, other).wait_recv()
-    blocks = join(rvec.at[n - 1], rinfo.at[n - 1], False)
+    blocks = join(rvec.at[n - 1], rinfo.at[n - 1], False, vec_copy(n - 1, other))
 
     def rows_copy(c, slot_r, which):
         return pltpu.make_async_remote_copy(

time: 28.8 us -> 28.8 us (level)
  no operation moved by 1% of the time
where the time goes in v3:
time: 28.8 us; the launch traced here: 28.7 us
  Pallas kernels  28.1 us (98%)
  between operations  0.64 us (2%)
    pallas_call x1, Pallas kernels, per_device(): pl.pallas_call(functools.partial(kernel, n, doms, cap, order), out_shape=...  27.3 us
    pallas_call x1, Pallas kernels, per_device(): pl.pallas_call(place, out_shape=(shapes[0], jax.ShapeDtypeStruct((R, per)...  0.78 us

profile of v3, /device:TPU:24, one launch (start us, length us, event | category | flops | bytes accessed | tf_op | source)
XLA Modules:
  0.0 28.7 jit_solution(17384495521957228717)
XLA Ops:
  0.6 27.3 %shard_map.67 = (bf16[256,768]{1,0:T(8,128)(2,1)S(1)}, bf16[64,256]{1,0:T(8,128)(2,1)S(1)}) custom-call(bf16[256,768]{1,0:T(8,128)(2,1)} %bitcast.12, s32[1,256]{1,0:T(1,128)} %bitcast.14, s32[32,256]{1,0:T(8,128)} %bitcast.13, s32[1,256]{1,0:T(1,128)} %refs_3_.1), custom_call_target="tpu_custom_call" | custom-call | tf_op jit(solution)/shard_map/pallas_call | solution.py:482
  27.9 0.8 %shard_map.68 = (bf16[256,768]{1,0:T(8,128)(2,1)}, bf16[32,256]{1,0:T(8,128)(2,1)}, bf16[32,256]{1,0:T(8,128)(2,1)}) custom-call(bf16[256,768]{1,0:T(8,128)(2,1)S(1)} %get-tuple-element.8.found_vec, bf16[64,256]{1,0:T(8,128)(2,1)S(1)} %get-tuple-element.9.found_rows), custom_call_target="tpu_custom_call" | custom-call | tf_op jit(solution)/shard_map/pallas_call | solution.py:516
